TPU v7x, 256 devices: a whole 4x4x8 slice. The times are simulated.
256 devices in a mesh: samp: 16 (over z_hi, x, core), gene: 4 (over z_lo), snp: 4 (over y).
Axes of the slice: x: 4, y: 4, z: 8 (z_hi: 2, z_lo: 4; z = z_hi * 4 + z_lo), core: 2. Of those that a mesh axis runs over, the one named last changes fastest.
Arguments:
- expression: bfloat16 [4096, 16384], P('samp', ('gene', 'snp')), may hold values from -6 to 6
- loadings: bfloat16 [16384, 128], P(('gene', 'snp')), may hold values from -0.046875 to 0.046875
- dosage: bfloat16 [4096, 16384], P(None, ('gene', 'snp')), may hold values from 0 to 2
Outputs:
- assoc: bfloat16 [16, 16, 64, 16384], P(None, 'samp', None, ('gene', 'snp'))
All inputs are finite; a program needn't handle non-finite values.
Results may differ from a plain program's by a relative error of at most 0.0065.
Values may be sent and summed in bfloat16 or wider, within the bound.
No kernel may reach another device: no remote copies, remote signals or barrier semaphores. Data moves between devices by JAX's collectives and lax.ppermute only.
A program may use at most 64 MiB of HBM per device.

v0:
```python
import jax
import jax.numpy as jnp
from jax import lax
from jax.sharding import PartitionSpec as P

ridge_factor = 1.0
ridge_sample = 1.0


def body(expression, loadings, dosage):
    contract = (((0,), (0,)), ((), ()))
    factor_count = loadings.shape[1]
    identity = jnp.eye(factor_count, dtype=jnp.float32)
    panel_genes = expression.shape[1] // lax.axis_size("samp")
    all_samples = dosage.shape[0]
    snp_count = dosage.shape[1]
    block_count = lax.axis_size("gene") * lax.axis_size("snp")
    norm_scale = 1.0 / jnp.sqrt(jnp.float32(all_samples))
    local_factor = jnp.dot(expression, loadings, preferred_element_type=jnp.float32)
    local_gram = lax.dot_general(loadings, loadings, contract, preferred_element_type=jnp.float32)
    factor_sum, gram_sum = lax.psum((local_factor, local_gram), ("gene", "snp"))
    lower_gram = jnp.linalg.cholesky(gram_sum + ridge_factor * identity)
    factors = jax.scipy.linalg.cho_solve((lower_gram, True), factor_sum.T).T.astype(jnp.bfloat16)
    local_hess = lax.dot_general(factors, factors, contract, preferred_element_type=jnp.float32)
    local_cross = lax.dot_general(factors, expression, contract, preferred_element_type=jnp.float32)
    hess_sum, cross_sum = lax.psum((local_hess, local_cross), "samp")
    lower_hess = jnp.linalg.cholesky(hess_sum + ridge_sample * identity)
    fit_coef = jax.scipy.linalg.cho_solve((lower_hess, True), cross_sum).astype(jnp.bfloat16)
    fitted = lax.dot_general(
        fit_coef, factors, (((0,), (1,)), ((), ())), preferred_element_type=jnp.float32
    )
    residual_t = (expression.T.astype(jnp.float32) - fitted).astype(jnp.bfloat16)
    panel_resid = lax.all_to_all(residual_t, "samp", split_axis=0, concat_axis=1, tiled=True)
    totals = (
        jnp.dot(
            lax.all_gather(panel_resid, ("gene", "snp"), axis=0, tiled=True),
            dosage,
            preferred_element_type=jnp.float32,
        )
        * norm_scale
    )
    return totals.astype(jnp.bfloat16).reshape(block_count, 1, panel_genes, snp_count)


def solution(mesh):
    placed = (P("samp", ("gene", "snp")), P(("gene", "snp"), None), P(None, ("gene", "snp")))
    return jax.shard_map(
        body,
        mesh=mesh,
        in_specs=placed,
        out_specs=P(None, "samp", None, ("gene", "snp")),
        check_vma=False,
    )
```

profile of v0, /device:TPU:1, one launch (start us, length us, event | category | flops | bytes accessed | tf_op | source)
XLA Modules:
  0.0 548.4 jit_solution(741673774838986686)
XLA Ops:
  6.5 0.0 copy-start
  6.5 0.0 all-reduce.5.cloned.1.call-start
  6.5 0.9 copy-done
  7.5 0.9 fusion.13
  8.4 2.0 fusion.14
  10.4 0.0 all-reduce.5.cloned.1.call-update
  10.4 0.0 all-reduce.7.cloned.1.call-start
  10.4 148.5 %all-reduce.5.cloned.1.call-done = (f32[256,128]{1,0:T(8,128)}, f32[128,128]{0,1:T(8,128)}) async-done(((f32[256,128]{1,0:T(8,128)}, f32[128,128]{0,1:T(8,128)}), (f32[256,128]{1,0:T(8,128)}, f32[128,128]{0,1:T(8,128)})) %all-reduce.5.cloned.1.call-update) | async-done | bytes 196624 | tf_op jit(solution)/shard_map/psum | solution.py:21
  159.0 0.9 convert_add_fusion.1
  159.8 0.1 copy.19
  159.9 0.9 fusion.10
  160.8 11.7 %cholesky.44 = f32[128,128]{1,0:T(8,128)S(1)} custom-call(f32[128,128]{1,0:T(8,128)S(1)} %fusion.10), custom_call_target="Cholesky" | custom-call | tf_op jit(solution)/shard_map/jit(cholesky)/cholesky | solution.py:22
  172.5 0.6 compare_reduce_fusion.1
  173.2 0.7 fusion.1
  173.8 9.8 %custom-call.16 = f32[1,128,128]{1,2,0:T(8,128)S(1)} custom-call(f32[1,128,128]{2,1,0:T(8,128)S(1)} %fusion.1), custom_call_target="InvertDiagBlocksLowerTriangular" | custom-call | tf_op jit(solution)/shard_map/jit(_cho_solve)/triangular_solve | solution.py:23
  183.6 1.2 fusion.8
  184.9 0.4 convolution_convert_fusion.1
  185.3 0.8 fusion.15
  186.1 2.1 fusion.16
  188.2 0.0 all-reduce.7.cloned.1.call-update
  188.2 0.2 all-gather.2.cloned.1.call-start
  188.4 1.2 copy.17
  189.7 183.0 %all-reduce.7.cloned.1.call-done = (f32[128,1024]{1,0:T(8,128)}, f32[128,128]{0,1:T(8,128)}) async-done(((f32[128,1024]{1,0:T(8,128)}, f32[128,128]{0,1:T(8,128)}), (f32[128,1024]{1,0:T(8,128)}, f32[128,128]{0,1:T(8,128)})) %all-reduce.7.cloned.1.call-update) | async-done | bytes 589840 | tf_op jit(solution)/shard_map/psum | solution.py:26
  372.7 0.9 convert_add_fusion
  373.5 0.1 copy.21
  373.6 0.9 fusion.6
  374.5 11.7 %cholesky.55 = f32[128,128]{1,0:T(8,128)S(1)} custom-call(f32[128,128]{1,0:T(8,128)S(1)} %fusion.6), custom_call_target="Cholesky" | custom-call | tf_op jit(solution)/shard_map/jit(cholesky)/cholesky | solution.py:27
  386.3 0.6 compare_reduce_fusion
  386.9 0.7 fusion.2
  387.6 9.8 %custom-call.17 = f32[1,128,128]{1,2,0:T(8,128)S(1)} custom-call(f32[1,128,128]{2,1,0:T(8,128)S(1)} %fusion.2), custom_call_target="InvertDiagBlocksLowerTriangular" | custom-call | tf_op jit(solution)/shard_map/jit(_cho_solve)/triangular_solve | solution.py:28
  397.4 1.7 fusion.4
  399.0 0.6 convolution_convert_fusion
  399.6 0.3 fusion
  400.0 21.6 %all_to_all.19 = bf16[16,64,256]{2,1,0:T(8,128)(2,1)S(1)} all-to-all(bf16[16,64,256]{2,1,0:T(8,128)(2,1)S(1)} %bitcast.48), channel_id=1, replica_groups=mesh['samp'=16,'gene'=4,'snp'=4] {'samp'}, dimensions={0} | all-to-all | bytes 1048576 | tf_op jit(solution)/shard_map/all_to_all | solution.py:33
  421.6 0.8 copy.26
  422.4 0.0 all-gather.2.cloned.1.call-update
  422.5 104.8 %all-gather.2.cloned.1.call-done = bf16[1024,4096]{1,0:T(8,128)(2,1)} async-done(((bf16[64,4096]{1,0:T(8,128)(2,1)}), bf16[1024,4096]{1,0:T(8,128)(2,1)}) %all-gather.2.cloned.1.call-update) | async-done | bytes 8388624 | tf_op jit(solution)/shard_map/all_gather | solution.py:36
  527.3 14.6 %multiply_convert_fusion = bf16[1024,1024]{1,0:T(8,128)(2,1)} fusion(bf16[1024,4096]{1,0:T(8,128)(2,1)} %all-gather.2.cloned.1.call-done, bf16[4096,1024]{1,0:T(8,128)(2,1)} %param.6), kind=kOutput, calls=%fused_computation | convolution fusion | flops 8592031744 | bytes 18874368 | tf_op jit(solution)/shard_map/dot_general | solution.py:35
  (2 shorter events, 0.1 us)
Async XLA Ops:
  6.5 1.0 copy-start
  6.5 152.4 %all-reduce.5.cloned.1.call-start = ((), (), s32[]{:S(2)}) async-start(), calls=%async_computation.2 | async-start | bytes 393216 | tf_op jit(solution)/shard_map/psum | solution.py:21
  10.4 362.3 %all-reduce.7.cloned.1.call-start = ((), (), s32[]{:S(2)}) async-start(), calls=%async_computation.3 | async-start | bytes 1179648 | tf_op jit(solution)/shard_map/psum | solution.py:26
  188.2 339.1 %all-gather.2.cloned.1.call-start = ((), (), s32[]{:S(2)}) async-start(), calls=%async_computation.1 | async-start | bytes 8912896 | tf_op jit(solution)/shard_map/all_gather | solution.py:36
Sparse Core Ops, SparseCore 0:
  10.5 148.4 all-reduce.4
  188.3 184.3 all-reduce.6
  422.6 104.6 all-gather.1
where the time goes:
time: 549 us; the launch traced here: 548 us
  waiting for transfers between devices  436 us (79%)
  other arithmetic  49.1 us (9%)
  matrix products  24.6 us (4%)
  blocking collectives  21.6 us (4%)
  between operations  13.2 us (2%)
    psum x1, waiting for transfers between devices, body(): hess_sum, cross_sum = lax.psum((local_hess, local_cross), 'samp')  183 us
    psum x1, waiting for transfers between devices, body(): factor_sum, gram_sum = lax.psum((local_factor, local_gram), ('gene', 'snp'))  149 us
    all_gather x1, waiting for transfers between devices, body(): lax.all_gather(panel_resid, ('gene', 'snp'), axis=0, tiled=True)  105 us
    all_to_all x1, blocking collectives, body(): lax.all_to_all(residual_t, 'samp', split_axis=0, concat_axis=1, tiled=True)  21.6 us
    dot_general x1, matrix products, body(): jnp.dot(lax.all_gather(panel_resid, ('gene', 'snp'), axis=0, tiled=True),...  14.6 us
    another operation x3, other arithmetic, body(): lower_hess = jnp.linalg.cholesky(hess_sum + ridge_sample * identity)  12.4 us
    another operation x3, other arithmetic, body(): lower_gram = jnp.linalg.cholesky(gram_sum + ridge_factor * identity)  12.4 us
  transfers between devices with their start and end apart: 3, of which 3 were waited for; matrix products, arithmetic and copies ran while one was open for 0% of the time, Pallas kernels for 0%

commit v1 on v0

--- a/solution.py
+++ b/solution.py
@@ -18,7 +18,7 @@
     norm_scale = 1.0 / jnp.sqrt(jnp.float32(all_samples))
     local_factor = jnp.dot(expression, loadings, preferred_element_type=jnp.float32)
     local_gram = lax.dot_general(loadings, loadings, contract, preferred_element_type=jnp.float32)
-    factor_sum, gram_sum = lax.psum((local_factor, local_gram), ("gene", "snp"))
+    factor_sum, gram_sum = lax.psum(lax.psum((local_factor, local_gram), "snp"), "gene")
     lower_gram = jnp.linalg.cholesky(gram_sum + ridge_factor * identity)
     factors = jax.scipy.linalg.cho_solve((lower_gram, True), factor_sum.T).T.astype(jnp.bfloat16)
     local_hess = lax.dot_general(factors, factors, contract, preferred_element_type=jnp.float32)

time: 549 us -> 493 us (0.90)
  waiting for transfers between devices: 436 us -> 381 us
    psum x1 -> x2, waiting for transfers between devices: 149 us -> 101 us  [the longest x1 52.3 us: body(): lax.psum(lax.psum((local_factor, local_gram), 'snp'), 'gene')]
    psum x1, waiting for transfers between devices: 183 us -> 175 us  [body(): hess_sum, cross_sum = lax.psum((local_hess, local_cross), 'samp')]
  transfers between devices with their start and end apart: 3 -> 4, of which waited for: 3 -> 4; matrix products, arithmetic and copies ran while one was open for 0% -> 0% of each run, Pallas kernels for 0% -> 0%
where the time goes in v1:
time: 493 us
  waiting for transfers between devices  381 us (77%)
  other arithmetic  49.1 us (10%)
  matrix products  24.6 us (5%)
  blocking collectives  21.6 us (4%)
  between operations  13.2 us (3%)
    psum x1, waiting for transfers between devices, body(): hess_sum, cross_sum = lax.psum((local_hess, local_cross), 'samp')  175 us
    all_gather x1, waiting for transfers between devices, body(): lax.all_gather(panel_resid, ('gene', 'snp'), axis=0, tiled=True)  105 us
    psum x1, waiting for transfers between devices, body(): lax.psum(lax.psum((local_factor, local_gram), 'snp'), 'gene')  52.3 us
    psum x1, waiting for transfers between devices, body(): lax.psum((local_factor, local_gram), 'snp')  48.6 us
    all_to_all x1, blocking collectives, body(): lax.all_to_all(residual_t, 'samp', split_axis=0, concat_axis=1, tiled=True)  21.6 us
    dot_general x1, matrix products, body(): jnp.dot(lax.all_gather(panel_resid, ('gene', 'snp'), axis=0, tiled=True),...  14.6 us
    another operation x3, other arithmetic, body(): lower_gram = jnp.linalg.cholesky(gram_sum + ridge_factor * identity)  12.4 us
    another operation x3, other arithmetic, body(): lower_hess = jnp.linalg.cholesky(hess_sum + ridge_sample * identity)  12.4 us
  transfers between devices with their start and end apart: 4, of which 4 were waited for; matrix products, arithmetic and copies ran while one was open for 0% of the time, Pallas kernels for 0%

profile of v1, /device:TPU:1, one launch (start us, length us, event | category | flops | bytes accessed | tf_op | source)
XLA Modules:
  0.0 492.8 jit_solution(3611915984451497624)
XLA Ops:
  6.5 0.0 copy-start
  6.5 0.0 all-reduce.9.cloned.1.call-start
  6.5 0.9 copy-done
  7.5 0.9 fusion.13
  8.4 2.0 fusion.14
  10.4 0.0 all-reduce.9.cloned.1.call-update
  10.4 0.0 all-reduce.11.cloned.1.call-start
  10.4 48.6 %all-reduce.9.cloned.1.call-done = (f32[256,128]{1,0:T(8,128)}, f32[128,128]{0,1:T(8,128)}) async-done(((f32[256,128]{1,0:T(8,128)}, f32[128,128]{0,1:T(8,128)}), (f32[256,128]{1,0:T(8,128)}, f32[128,128]{0,1:T(8,128)})) %all-reduce.9.cloned.1.call-update) | async-done | bytes 196624 | tf_op jit(solution)/shard_map/psum | solution.py:21
  59.0 0.0 all-reduce.11.cloned.1.call-update
  59.0 0.0 all-reduce.7.cloned.1.call-start
  59.1 52.3 %all-reduce.11.cloned.1.call-done = (f32[256,128]{1,0:T(8,128)}, f32[128,128]{0,1:T(8,128)}) async-done(((f32[256,128]{1,0:T(8,128)}, f32[128,128]{0,1:T(8,128)}), (f32[256,128]{1,0:T(8,128)}, f32[128,128]{0,1:T(8,128)})) %all-reduce.11.cloned.1.call-update) | async-done | bytes 196624 | tf_op jit(solution)/shard_map/psum | solution.py:21
  111.4 0.9 convert_add_fusion.1
  112.2 0.1 copy.19
  112.3 0.9 fusion.10
  113.2 11.7 %cholesky.44 = f32[128,128]{1,0:T(8,128)S(1)} custom-call(f32[128,128]{1,0:T(8,128)S(1)} %fusion.10), custom_call_target="Cholesky" | custom-call | tf_op jit(solution)/shard_map/jit(cholesky)/cholesky | solution.py:22
  124.9 0.6 compare_reduce_fusion.1
  125.6 0.7 fusion.1
  126.2 9.8 %custom-call.16 = f32[1,128,128]{1,2,0:T(8,128)S(1)} custom-call(f32[1,128,128]{2,1,0:T(8,128)S(1)} %fusion.1), custom_call_target="InvertDiagBlocksLowerTriangular" | custom-call | tf_op jit(solution)/shard_map/jit(_cho_solve)/triangular_solve | solution.py:23
  136.1 1.2 fusion.8
  137.3 0.4 convolution_convert_fusion.1
  137.7 0.8 fusion.15
  138.5 2.1 fusion.16
  140.6 0.0 all-reduce.7.cloned.1.call-update
  140.6 0.2 all-gather.2.cloned.1.call-start
  140.9 1.2 copy.17
  142.1 175.0 %all-reduce.7.cloned.1.call-done = (f32[128,1024]{1,0:T(8,128)}, f32[128,128]{0,1:T(8,128)}) async-done(((f32[128,1024]{1,0:T(8,128)}, f32[128,128]{0,1:T(8,128)}), (f32[128,1024]{1,0:T(8,128)}, f32[128,128]{0,1:T(8,128)})) %all-reduce.7.cloned.1.call-update) | async-done | bytes 589840 | tf_op jit(solution)/shard_map/psum | solution.py:26
  317.1 0.9 convert_add_fusion
  317.9 0.1 copy.21
  318.0 0.9 fusion.6
  318.9 11.7 %cholesky.55 = f32[128,128]{1,0:T(8,128)S(1)} custom-call(f32[128,128]{1,0:T(8,128)S(1)} %fusion.6), custom_call_target="Cholesky" | custom-call | tf_op jit(solution)/shard_map/jit(cholesky)/cholesky | solution.py:27
  330.6 0.6 compare_reduce_fusion
  331.3 0.7 fusion.2
  331.9 9.8 %custom-call.17 = f32[1,128,128]{1,2,0:T(8,128)S(1)} custom-call(f32[1,128,128]{2,1,0:T(8,128)S(1)} %fusion.2), custom_call_target="InvertDiagBlocksLowerTriangular" | custom-call | tf_op jit(solution)/shard_map/jit(_cho_solve)/triangular_solve | solution.py:28
  341.8 1.7 fusion.4
  343.4 0.6 convolution_convert_fusion
  344.0 0.3 fusion
  344.4 21.6 %all_to_all.19 = bf16[16,64,256]{2,1,0:T(8,128)(2,1)S(1)} all-to-all(bf16[16,64,256]{2,1,0:T(8,128)(2,1)S(1)} %bitcast.48), channel_id=1, replica_groups=mesh['samp'=16,'gene'=4,'snp'=4] {'samp'}, dimensions={0} | all-to-all | bytes 1048576 | tf_op jit(solution)/shard_map/all_to_all | solution.py:33
  366.0 0.8 copy.26
  366.8 0.0 all-gather.2.cloned.1.call-update
  366.8 104.8 %all-gather.2.cloned.1.call-done = bf16[1024,4096]{1,0:T(8,128)(2,1)} async-done(((bf16[64,4096]{1,0:T(8,128)(2,1)}), bf16[1024,4096]{1,0:T(8,128)(2,1)}) %all-gather.2.cloned.1.call-update) | async-done | bytes 8388624 | tf_op jit(solution)/shard_map/all_gather | solution.py:36
  471.7 14.6 %multiply_convert_fusion = bf16[1024,1024]{1,0:T(8,128)(2,1)} fusion(bf16[1024,4096]{1,0:T(8,128)(2,1)} %all-gather.2.cloned.1.call-done, bf16[4096,1024]{1,0:T(8,128)(2,1)} %param.6), kind=kOutput, calls=%fused_computation | convolution fusion | flops 8592031744 | bytes 18874368 | tf_op jit(solution)/shard_map/dot_general | solution.py:35
  (2 shorter events, 0.1 us)
Async XLA Ops:
  6.5 1.0 copy-start
  6.5 52.5 %all-reduce.9.cloned.1.call-start = ((), (), s32[]{:S(2)}) async-start(), calls=%async_computation.3 | async-start | bytes 393216 | tf_op jit(solution)/shard_map/psum | solution.py:21
  10.4 101.0 %all-reduce.11.cloned.1.call-start = ((), (), s32[]{:S(2)}) async-start(), calls=%async_computation.4 | async-start | bytes 393216 | tf_op jit(solution)/shard_map/psum | solution.py:21
  59.0 258.0 %all-reduce.7.cloned.1.call-start = ((), (), s32[]{:S(2)}) async-start(), calls=%async_computation.2 | async-start | bytes 1179648 | tf_op jit(solution)/shard_map/psum | solution.py:26
  140.6 331.0 %all-gather.2.cloned.1.call-start = ((), (), s32[]{:S(2)}) async-start(), calls=%async_computation.1 | async-start | bytes 8912896 | tf_op jit(solution)/shard_map/all_gather | solution.py:36
Sparse Core Ops, SparseCore 0:
  10.5 48.4 all-reduce.8
  61.7 49.6 all-reduce.10
  140.7 176.2 all-reduce.6
  367.0 104.6 all-gather.1

commit v2 on v0

--- a/solution.py
+++ b/solution.py
@@ -33,7 +33,12 @@
     panel_resid = lax.all_to_all(residual_t, "samp", split_axis=0, concat_axis=1, tiled=True)
     totals = (
         jnp.dot(
-            lax.all_gather(panel_resid, ("gene", "snp"), axis=0, tiled=True),
+            jnp.concatenate(
+                lax.all_to_all(
+                    jnp.stack([panel_resid] * lax.axis_size(("gene", "snp"))), ("gene", "snp"), 0, 0
+                ),
+                axis=0,
+            ),
             dosage,
             preferred_element_type=jnp.float32,
         )

time: 549 us -> 635 us (1.16)
  blocking collectives: 21.6 us -> 216 us
  waiting for transfers between devices: 436 us -> 332 us
    all_to_all x0 -> x1, blocking collectives: none -> 194 us  [body(): lax.all_to_all(jnp.stack([panel_resid] * lax.axis_size(('gene', 'snp'))),...]
    all_gather x1 -> x0, waiting for transfers between devices: 105 us -> none  [body(): lax.all_gather(panel_resid, ('gene', 'snp'), axis=0, tiled=True)]
  transfers between devices with their start and end apart: 3 -> 2, of which waited for: 3 -> 2; matrix products, arithmetic and copies ran while one was open for 0% -> 0% of each run, Pallas kernels for 0% -> 0%
where the time goes in v2:
time: 635 us; the launch traced here: 634 us
  waiting for transfers between devices  332 us (52%)
  blocking collectives  216 us (34%)
  other arithmetic  49.3 us (8%)
  matrix products  20 us (3%)
  between operations  13.5 us (2%)
    all_to_all x1, blocking collectives, body(): lax.all_to_all(jnp.stack([panel_resid] * lax.axis_size(('gene', 'snp'))),...  194 us
    psum x1, waiting for transfers between devices, body(): hess_sum, cross_sum = lax.psum((local_hess, local_cross), 'samp')  183 us
    psum x1, waiting for transfers between devices, body(): factor_sum, gram_sum = lax.psum((local_factor, local_gram), ('gene', 'snp'))  149 us
    all_to_all x1, blocking collectives, body(): lax.all_to_all(residual_t, 'samp', split_axis=0, concat_axis=1, tiled=True)  21.6 us
  transfers between devices with their start and end apart: 2, of which 2 were waited for; matrix products, arithmetic and copies ran while one was open for 0% of the time, Pallas kernels for 0%

profile of v2, /device:TPU:1, one launch (start us, length us, event | category | flops | bytes accessed | tf_op | source)
XLA Modules:
  0.0 634.2 jit_solution(14797989725246243701)
XLA Ops:
  6.5 0.0 copy-start
  6.5 0.0 all-reduce.5.cloned.1.call-start
  6.5 0.9 copy-done
  7.5 0.9 fusion.13
  8.4 2.0 fusion.14
  10.4 0.0 all-reduce.5.cloned.1.call-update
  10.4 0.0 all-reduce.7.cloned.1.call-start
  10.4 148.5 %all-reduce.5.cloned.1.call-done = (f32[256,128]{1,0:T(8,128)}, f32[128,128]{0,1:T(8,128)}) async-done(((f32[256,128]{1,0:T(8,128)}, f32[128,128]{0,1:T(8,128)}), (f32[256,128]{1,0:T(8,128)}, f32[128,128]{0,1:T(8,128)})) %all-reduce.5.cloned.1.call-update) | async-done | bytes 196624 | tf_op jit(solution)/shard_map/psum | solution.py:21
  159.0 0.9 convert_add_fusion.1
  159.8 0.1 copy.19
  159.9 0.9 fusion.10
  160.8 11.7 %cholesky.44 = f32[128,128]{1,0:T(8,128)S(1)} custom-call(f32[128,128]{1,0:T(8,128)S(1)} %fusion.10), custom_call_target="Cholesky" | custom-call | tf_op jit(solution)/shard_map/jit(cholesky)/cholesky | solution.py:22
  172.5 0.6 compare_reduce_fusion.1
  173.2 0.7 fusion.1
  173.8 9.8 %custom-call.16 = f32[1,128,128]{1,2,0:T(8,128)S(1)} custom-call(f32[1,128,128]{2,1,0:T(8,128)S(1)} %fusion.1), custom_call_target="InvertDiagBlocksLowerTriangular" | custom-call | tf_op jit(solution)/shard_map/jit(_cho_solve)/triangular_solve | solution.py:23
  183.6 1.2 fusion.8
  184.9 0.4 convolution_convert_fusion.1
  185.3 0.8 fusion.15
  186.1 2.1 fusion.16
  188.2 0.0 all-reduce.7.cloned.1.call-update
  188.2 1.2 copy.17
  189.5 183.2 %all-reduce.7.cloned.1.call-done = (f32[128,1024]{1,0:T(8,128)}, f32[128,128]{0,1:T(8,128)}) async-done(((f32[128,1024]{1,0:T(8,128)}, f32[128,128]{0,1:T(8,128)}), (f32[128,1024]{1,0:T(8,128)}, f32[128,128]{0,1:T(8,128)})) %all-reduce.7.cloned.1.call-update) | async-done | bytes 589840 | tf_op jit(solution)/shard_map/psum | solution.py:26
  372.7 0.9 convert_add_fusion
  373.5 0.1 copy.21
  373.6 0.9 fusion.6
  374.5 11.7 %cholesky.55 = f32[128,128]{1,0:T(8,128)S(1)} custom-call(f32[128,128]{1,0:T(8,128)S(1)} %fusion.6), custom_call_target="Cholesky" | custom-call | tf_op jit(solution)/shard_map/jit(cholesky)/cholesky | solution.py:27
  386.3 0.6 compare_reduce_fusion
  386.9 0.7 fusion.2
  387.6 9.9 %custom-call.17 = f32[1,128,128]{1,2,0:T(8,128)S(1)} custom-call(f32[1,128,128]{2,1,0:T(8,128)S(1)} %fusion.2), custom_call_target="InvertDiagBlocksLowerTriangular" | custom-call | tf_op jit(solution)/shard_map/jit(_cho_solve)/triangular_solve | solution.py:28
  397.5 1.7 fusion.4
  399.2 0.6 convolution_convert_fusion
  399.8 0.3 fusion
  400.1 21.6 %all_to_all.21 = bf16[16,64,256]{2,1,0:T(8,128)(2,1)S(1)} all-to-all(bf16[16,64,256]{2,1,0:T(8,128)(2,1)S(1)} %bitcast.50), channel_id=1, replica_groups=mesh['samp'=16,'gene'=4,'snp'=4] {'samp'}, dimensions={0} | all-to-all | bytes 1048576 | tf_op jit(solution)/shard_map/all_to_all | solution.py:33
  421.8 0.0 slice-start
  421.8 1.1 stack.5
  422.9 0.0 slice-start.1
  422.9 194.4 %all_to_all.22 = bf16[16,64,4096]{2,1,0:T(8,128)(2,1)S(1)} all-to-all(bf16[16,64,4096]{2,1,0:T(8,128)(2,1)S(1)} %stack.5), channel_id=1, replica_groups=mesh['samp'=16,'gene'=4,'snp'=4] {'gene','snp'}, dimensions={0} | all-to-all | bytes 16777216 | tf_op jit(solution)/shard_map/all_to_all | solution.py:37
  617.3 0.0 slice-done
  617.3 0.0 slice-done.1
  617.3 10.0 %multiply_convert_fusion = bf16[1024,1024]{1,0:T(8,128)(2,1)} fusion(bf16[1024,4096]{1,0:T(8,128)(2,1)S(1)} %bitcast.48, bf16[4096,1024]{1,0:T(8,128)(2,1)S(1)} %bitcast.53), kind=kOutput, calls=%fused_computation | convolution fusion | flops 8592031744 | bytes 18874368 | tf_op jit(solution)/shard_map/dot_general | solution.py:35
  (4 shorter events, 0.1 us)
Async XLA Ops:
  6.5 1.0 copy-start
  6.5 152.4 %all-reduce.5.cloned.1.call-start = ((), (), s32[]{:S(2)}) async-start(), calls=%async_computation.2 | async-start | bytes 393216 | tf_op jit(solution)/shard_map/psum | solution.py:21
  10.4 362.3 %all-reduce.7.cloned.1.call-start = ((), (), s32[]{:S(2)}) async-start(), calls=%async_computation.3 | async-start | bytes 1179648 | tf_op jit(solution)/shard_map/psum | solution.py:26
  421.8 195.5 %slice-start = ((s8[8388608]{0:T(1024)(128)(4,1)}), s8[4194304]{0:T(1024)(128)(4,1)S(1)}, s32[]{:S(2)}) async-start(s8[8388608]{0:T(1024)(128)(4,1)} %bitcast.52), calls=%async_computation.4 | async-start | bytes 8388608
  422.9 194.5 %slice-start.1 = ((s8[8388608]{0:T(1024)(128)(4,1)}), s8[4194304]{0:T(1024)(128)(4,1)S(1)}, s32[]{:S(2)}) async-start(s8[8388608]{0:T(1024)(128)(4,1)} %bitcast.52), calls=%async_computation.5 | async-start | bytes 8388608
Sparse Core Ops, SparseCore 0:
  10.5 148.4 all-reduce.4
  188.3 184.3 all-reduce.6
